TPU v7x, 512 devices: a whole 4x8x8 slice. The times are simulated.
512 devices in a mesh: temp: 32 (over y, x), bond: 16 (over z, core).
Axes of the slice: x: 4, y: 8, z: 8, core: 2. Of those that a mesh axis runs over, the one named last changes fastest.
Arguments:
- tensor: float32 [2048, 4096], P(('temp', 'bond')), parts along dimension 0, may hold values from -6 to 6
- isometries: float32 [96, 64, 4096], P('temp', 'bond'), parts along dimension 0, may hold values from -0.09375 to 0.09375
Outputs:
- final_tensor: float32 [2048, 4096], P(('temp', 'bond')), parts along dimension 0
- log_density: float32 [32], P('temp'), parts along dimension 0
There are 32 independent parts, one for each index of `temp`. A program takes and returns all parts, laid end to end along the dimension named above; each array names one. Nothing has to cross between parts.
All inputs are finite; a program needn't handle non-finite values. Where the computation divides by a largest or mean magnitude, that divisor is 1e-20 or more.
Results may differ from a plain program's by a relative error of at most 0.00027.
Values sent between devices are 32-bit elements; how exact they have to be, the bound alone decides.
A program may use at most 64 MiB of HBM per device.

v0:
```python
import jax
import jax.numpy as jnp
from jax import lax
from jax.sharding import PartitionSpec as P

PRECISE = lax.Precision.HIGHEST
EPSILON = 1e-06


def laid_out(pieces, dim):
    pieces = jnp.moveaxis(pieces, 0, dim)
    dims = pieces.shape
    return pieces.reshape(*dims[:dim], dims[dim] * dims[dim + 1], *dims[dim + 2 :])


def copy_for_each(x, axis):
    devices = lax.axis_size(axis)
    return lax.all_to_all(jnp.broadcast_to(x[None], (devices, *x.shape)), axis, 0, 0, tiled=True)


def gather_directly(x, axis, dim):
    return laid_out(copy_for_each(x, axis), dim)


def of_everyone(x, axis):
    return copy_for_each(x, axis).max(axis=0)


def on_device(tensor, isometries):
    parts = lax.axis_size("bond")
    sections = isometries.shape[0]
    rows = tensor.shape[0]
    width = rows * parts
    log_density = jnp.zeros((1,), jnp.float32)
    own_part = tensor
    own_scale = jnp.ones((1, 1), jnp.float32)
    for section_idx in range(sections):
        prior_weight = 0.5**section_idx
        gathered, scales = (
            gather_directly(own_part, "bond", 0),
            gather_directly(own_scale, "bond", 0),
        )
        largest = jnp.max(scales)
        factors = jnp.repeat(scales[:, 0] / largest, rows)
        gathered = gathered * factors[:, None]
        if section_idx > 0:
            log_density = log_density + jnp.log(largest) * prior_weight
        current = gathered.reshape(width, width, width).transpose(1, 2, 0)
        isometry = isometries[section_idx].reshape(rows, width, width)
        inner_sum = jnp.einsum("bct,nst->nbcs", current, isometry, precision=PRECISE)
        summed = jnp.einsum("abs,nbcs->nac", current, inner_sum, precision=PRECISE)
        summed = summed.reshape(rows, width * width)
        local_peak = jnp.max(jnp.abs(summed))
        if section_idx + 1 < sections:
            own_scale = (local_peak + EPSILON).reshape(1, 1)
            own_part = summed / own_scale
        else:
            largest = of_everyone(local_peak, "bond") + EPSILON
            own_part = summed / largest
            log_density = log_density + jnp.log(largest) * 0.5 ** (section_idx + 1)
    return (own_part, log_density)


def solution(mesh):
    in_specs = (P(("temp", "bond"), None), P("temp", "bond", None))
    out_specs = (P(("temp", "bond"), None), P("temp"))
    return jax.shard_map(
        on_device, mesh=mesh, in_specs=in_specs, out_specs=out_specs, check_vma=False
    )
```

profile of v0, /device:TPU:1, one launch (start us, length us, event | category | flops | bytes accessed | tf_op | source)
XLA Modules:
  0.0 221.7 jit_solution(4912181132892076155)
XLA Ops:
  0.6 0.0 copy-start.3
  0.6 2.1 broadcast_in_dim.16
  2.7 11.8 %all-to-all-start = ((f32[16,4,4096]{2,1,0:T(4,128)}), f32[16,4,4096]{2,1,0:T(4,128)S(1)}, u32[]{:S(2)}, u32[]{:S(2)}) async-start(f32[16,4,4096]{2,1,0:T(4,128)} %broadcast_in_dim.16), calls=%async_computation | async-start | bytes 2097152 | tf_op jit(solution)/shard_map/all_to_all | solution.py:18
  14.5 0.0 copy-done.3
  14.6 0.1 reshape.82
  14.7 27.8 %all-to-all-done = f32[16,4,4096]{2,1,0:T(4,128)S(1)} async-done(((f32[16,4,4096]{2,1,0:T(4,128)}), f32[16,4,4096]{2,1,0:T(4,128)S(1)}, u32[]{:S(2)}, u32[]{:S(2)}) %all-to-all-start) | async-done | bytes 1048608 | tf_op jit(solution)/shard_map/all_to_all | solution.py:18
  42.5 1.0 reshape.78
  43.5 2.2 %copy.37 = f32[64,64,64]{0,2,1:T(8,128)} copy(f32[64,64,64]{2,1,0:T(8,128)S(1)} %reshape.78) | data formatting | bytes 2097152 | tf_op jit(solution)/shard_map/reshape | solution.py:13
  45.8 3.5 %copy.38 = f32[64,64,64]{2,0,1:T(8,128)} copy(f32[64,64,64]{1,0,2:T(8,128)S(1)} %bitcast.83) | data formatting | bytes 2097152 | tf_op jit(solution)/shard_map/transpose | solution.py:48
  49.3 0.0 copy-start
  49.3 8.6 %fusion.6 = f32[64,64,4,64]{3,1,0,2:T(8,128)S(1)} fusion(f32[64,64,64]{0,2,1:T(8,128)} %copy.37, f32[4,64,64,1]{2,1,0,3:T(8,128)S(1)} %reshape.82), kind=kOutput, calls=%fused_computation.6 | convolution fusion | flops 805306368 | bytes 5308416 | tf_op jit(solution)/shard_map/bct,nst->nbcs/dot_general | solution.py:50
  57.9 0.0 copy-done
  57.9 7.4 %abs_reduce_fusion.2 = (f32[]{:T(128)}, f32[4,64,64]{2,1,0:T(8,128)S(1)}) fusion(f32[64,64,64]{2,0,1:T(8,128)S(1)} %copy-done, f32[64,64,4,64]{3,1,0,2:T(8,128)S(1)} %fusion.6), kind=kOutput, calls=%fused_computation.28 | convolution fusion | flops 805339136 | bytes 5308420 | tf_op jit(solution)/shard_map/abs,nbcs->nac/dot_general | solution.py:51
  66.0 0.6 broadcast_in_dim.18
  66.6 3.4 %all-to-all-start.2 = ((f32[16,1,1]{2,1,0:T(1,128)}), f32[16,1,1]{2,1,0:T(1,128)S(1)}, u32[]{:S(2)}, u32[]{:S(2)}) async-start(f32[16,1,1]{2,1,0:T(1,128)} %broadcast_in_dim.18), calls=%async_computation.2 | async-start | bytes 16384 | tf_op jit(solution)/shard_map/all_to_all | solution.py:18
  70.1 0.1 copy.39
  70.2 0.1 div.72
  70.3 6.7 %all-to-all-done.2 = f32[16,1,1]{2,1,0:T(1,128)S(1)} async-done(((f32[16,1,1]{2,1,0:T(1,128)}), f32[16,1,1]{2,1,0:T(1,128)S(1)}, u32[]{:S(2)}, u32[]{:S(2)}) %all-to-all-start.2) | async-done | bytes 96 | tf_op jit(solution)/shard_map/all_to_all | solution.py:18
  77.0 1.2 broadcast_in_dim.17
  78.2 4.1 %all-to-all-start.1 = ((f32[16,4,4096]{2,1,0:T(4,128)}), f32[16,4,4096]{2,1,0:T(4,128)S(1)}, u32[]{:S(2)}, u32[]{:S(2)}) async-start(f32[16,4,4096]{2,1,0:T(4,128)} %broadcast_in_dim.17), calls=%async_computation.1 | async-start | bytes 2097152 | tf_op jit(solution)/shard_map/all_to_all | solution.py:18
  82.3 0.1 reshape.86
  82.4 0.6 reduce_max.59
  83.0 0.9 divide_reduce_fusion.1
  83.9 0.1 broadcast_in_dim.19
  84.0 0.1 mul.36
  84.1 26.3 %all-to-all-done.1 = f32[16,4,4096]{2,1,0:T(4,128)S(1)} async-done(((f32[16,4,4096]{2,1,0:T(4,128)}), f32[16,4,4096]{2,1,0:T(4,128)S(1)}, u32[]{:S(2)}, u32[]{:S(2)}) %all-to-all-start.1) | async-done | bytes 1048608 | tf_op jit(solution)/shard_map/all_to_all | solution.py:18
  110.3 2.4 %reshape.79 = f32[64,64,64]{2,1,0:T(8,128)} reshape(f32[16,4,4096]{2,1,0:T(4,128)S(1)} %all-to-all-done.1) | data formatting | bytes 2097152 | tf_op jit(solution)/shard_map/reshape | solution.py:13
  112.7 1.8 multiply_bitcast_fusion.1
  114.5 2.2 %copy.40 = f32[64,64,64]{2,1,0:T(8,128)} copy(f32[64,64,64]{1,0,2:T(8,128)S(1)} %multiply_bitcast_fusion.1) | data formatting | bytes 2097152 | tf_op jit(solution)/shard_map/transpose | solution.py:48
  116.7 3.1 %copy.41 = f32[64,64,64]{2,0,1:T(8,128)} copy(f32[64,64,64]{1,0,2:T(8,128)S(1)} %multiply_bitcast_fusion.1) | data formatting | bytes 2097152 | tf_op jit(solution)/shard_map/transpose | solution.py:48
  119.8 0.0 copy-start.1
  119.8 8.6 %fusion.12 = f32[64,64,4,64]{3,1,0,2:T(8,128)S(1)} fusion(f32[64,64,64]{2,1,0:T(8,128)} %copy.40, f32[4,64,64,1]{2,1,0,3:T(8,128)S(1)} %reshape.86), kind=kOutput, calls=%fused_computation.12 | convolution fusion | flops 805306368 | bytes 5308416 | tf_op jit(solution)/shard_map/bct,nst->nbcs/dot_general | solution.py:50
  128.4 0.0 copy-done.1
  128.4 7.7 %abs_reduce_fusion.1 = (f32[]{:T(128)}, f32[4,64,64]{2,1,0:T(8,128)S(1)}) fusion(f32[64,64,64]{2,0,1:T(8,128)S(1)} %copy-done.1, f32[64,64,4,64]{3,1,0,2:T(8,128)S(1)} %fusion.12), kind=kOutput, calls=%fused_computation.26 | convolution fusion | flops 805339136 | bytes 5308420 | tf_op jit(solution)/shard_map/abs,nbcs->nac/dot_general | solution.py:51
  136.7 0.6 broadcast_in_dim.21
  137.3 3.4 %all-to-all-start.4 = ((f32[16,1,1]{2,1,0:T(1,128)}), f32[16,1,1]{2,1,0:T(1,128)S(1)}, u32[]{:S(2)}, u32[]{:S(2)}) async-start(f32[16,1,1]{2,1,0:T(1,128)} %broadcast_in_dim.21), calls=%async_computation.4 | async-start | bytes 16384 | tf_op jit(solution)/shard_map/all_to_all | solution.py:18
  140.8 0.1 copy.42
  140.9 0.1 div.79
  141.0 6.7 %all-to-all-done.4 = f32[16,1,1]{2,1,0:T(1,128)S(1)} async-done(((f32[16,1,1]{2,1,0:T(1,128)}), f32[16,1,1]{2,1,0:T(1,128)S(1)}, u32[]{:S(2)}, u32[]{:S(2)}) %all-to-all-start.4) | async-done | bytes 96 | tf_op jit(solution)/shard_map/all_to_all | solution.py:18
  147.7 1.2 broadcast_in_dim.20
  148.9 4.1 %all-to-all-start.3 = ((f32[16,4,4096]{2,1,0:T(4,128)}), f32[16,4,4096]{2,1,0:T(4,128)S(1)}, u32[]{:S(2)}, u32[]{:S(2)}) async-start(f32[16,4,4096]{2,1,0:T(4,128)} %broadcast_in_dim.20), calls=%async_computation.3 | async-start | bytes 2097152 | tf_op jit(solution)/shard_map/all_to_all | solution.py:18
  153.0 0.1 reshape.90
  153.8 0.6 reduce_max.61
  155.2 0.9 divide_reduce_fusion
  156.0 0.1 broadcast_in_dim.22
  156.1 0.1 mul.39
  156.2 24.9 %all-to-all-done.3 = f32[16,4,4096]{2,1,0:T(4,128)S(1)} async-done(((f32[16,4,4096]{2,1,0:T(4,128)}), f32[16,4,4096]{2,1,0:T(4,128)S(1)}, u32[]{:S(2)}, u32[]{:S(2)}) %all-to-all-start.3) | async-done | bytes 1048608 | tf_op jit(solution)/shard_map/all_to_all | solution.py:18
  181.1 2.4 %reshape.80 = f32[64,64,64]{2,1,0:T(8,128)} reshape(f32[16,4,4096]{2,1,0:T(4,128)S(1)} %all-to-all-done.3) | data formatting | bytes 2097152 | tf_op jit(solution)/shard_map/reshape | solution.py:13
  183.4 1.8 multiply_bitcast_fusion
  185.2 2.2 %copy.43 = f32[64,64,64]{2,1,0:T(8,128)} copy(f32[64,64,64]{1,0,2:T(8,128)S(1)} %multiply_bitcast_fusion) | data formatting | bytes 2097152 | tf_op jit(solution)/shard_map/transpose | solution.py:48
  187.5 3.2 %copy.44 = f32[64,64,64]{2,0,1:T(8,128)} copy(f32[64,64,64]{1,0,2:T(8,128)S(1)} %multiply_bitcast_fusion) | data formatting | bytes 2097152 | tf_op jit(solution)/shard_map/transpose | solution.py:48
  190.7 0.0 copy-start.2
  190.7 8.6 %fusion.9 = f32[64,64,4,64]{3,1,0,2:T(8,128)S(1)} fusion(f32[64,64,64]{2,1,0:T(8,128)} %copy.43, f32[4,64,64,1]{2,1,0,3:T(8,128)S(1)} %reshape.90), kind=kOutput, calls=%fused_computation.9 | convolution fusion | flops 805306368 | bytes 5308416 | tf_op jit(solution)/shard_map/bct,nst->nbcs/dot_general | solution.py:50
  199.3 0.0 copy-done.2
  199.3 7.2 %abs_reduce_fusion = (f32[]{:T(128)}, f32[4,64,64]{2,1,0:T(8,128)S(1)}) fusion(f32[64,64,64]{2,0,1:T(8,128)S(1)} %copy-done.2, f32[64,64,4,64]{3,1,0,2:T(8,128)S(1)} %fusion.9), kind=kOutput, calls=%fused_computation.24 | convolution fusion | flops 805339136 | bytes 5308420 | tf_op jit(solution)/shard_map/abs,nbcs->nac/dot_general | solution.py:51
  206.5 1.2 broadcast_in_dim.23
  207.8 3.4 %all-to-all-start.5 = ((f32[16,1,1]{2,1,0:T(1,128)}), f32[16,1,1]{2,1,0:T(1,128)S(1)}, u32[]{:S(2)}, u32[]{:S(2)}) async-start(f32[16,1,1]{2,1,0:T(1,128)} %broadcast_in_dim.23), calls=%async_computation.5 | async-start | bytes 16384 | tf_op jit(solution)/shard_map/all_to_all | solution.py:18
  211.2 7.0 %all-to-all-done.5 = f32[16,1,1]{2,1,0:T(1,128)S(1)} async-done(((f32[16,1,1]{2,1,0:T(1,128)}), f32[16,1,1]{2,1,0:T(1,128)S(1)}, u32[]{:S(2)}, u32[]{:S(2)}) %all-to-all-start.5) | async-done | bytes 96 | tf_op jit(solution)/shard_map/all_to_all | solution.py:18
  218.2 0.6 reduce_max.63
  219.5 0.1 copy.46
  219.6 0.7 div.86
  (4 shorter events, 0.1 us)
Async XLA Ops:
  0.6 13.9 %copy-start.3 = (f32[3,4,4096]{2,1,0:T(4,128)S(1)}, f32[3,4,4096]{2,1,0:T(4,128)}, u32[]{:S(2)}) copy-start(f32[3,4,4096]{2,1,0:T(4,128)} %param.3) | copy-start | bytes 589828
  2.7 39.8 %all-to-all-start = ((f32[16,4,4096]{2,1,0:T(4,128)}), f32[16,4,4096]{2,1,0:T(4,128)S(1)}, u32[]{:S(2)}, u32[]{:S(2)}) async-start(f32[16,4,4096]{2,1,0:T(4,128)} %broadcast_in_dim.16), calls=%async_computation | async-start | bytes 2097152 | tf_op jit(solution)/shard_map/all_to_all | solution.py:18
  49.3 8.6 %copy-start = (f32[64,64,64]{2,0,1:T(8,128)S(1)}, f32[64,64,64]{2,0,1:T(8,128)}, u32[]{:S(2)}) copy-start(f32[64,64,64]{2,0,1:T(8,128)} %copy.38) | copy-start | bytes 3145732
  66.6 10.4 %all-to-all-start.2 = ((f32[16,1,1]{2,1,0:T(1,128)}), f32[16,1,1]{2,1,0:T(1,128)S(1)}, u32[]{:S(2)}, u32[]{:S(2)}) async-start(f32[16,1,1]{2,1,0:T(1,128)} %broadcast_in_dim.18), calls=%async_computation.2 | async-start | bytes 16384 | tf_op jit(solution)/shard_map/all_to_all | solution.py:18
  78.2 32.1 %all-to-all-start.1 = ((f32[16,4,4096]{2,1,0:T(4,128)}), f32[16,4,4096]{2,1,0:T(4,128)S(1)}, u32[]{:S(2)}, u32[]{:S(2)}) async-start(f32[16,4,4096]{2,1,0:T(4,128)} %broadcast_in_dim.17), calls=%async_computation.1 | async-start | bytes 2097152 | tf_op jit(solution)/shard_map/all_to_all | solution.py:18
  119.8 8.6 %copy-start.1 = (f32[64,64,64]{2,0,1:T(8,128)S(1)}, f32[64,64,64]{2,0,1:T(8,128)}, u32[]{:S(2)}) copy-start(f32[64,64,64]{2,0,1:T(8,128)} %copy.41) | copy-start | bytes 3145732
  137.3 10.4 %all-to-all-start.4 = ((f32[16,1,1]{2,1,0:T(1,128)}), f32[16,1,1]{2,1,0:T(1,128)S(1)}, u32[]{:S(2)}, u32[]{:S(2)}) async-start(f32[16,1,1]{2,1,0:T(1,128)} %broadcast_in_dim.21), calls=%async_computation.4 | async-start | bytes 16384 | tf_op jit(solution)/shard_map/all_to_all | solution.py:18
  148.9 32.1 %all-to-all-start.3 = ((f32[16,4,4096]{2,1,0:T(4,128)}), f32[16,4,4096]{2,1,0:T(4,128)S(1)}, u32[]{:S(2)}, u32[]{:S(2)}) async-start(f32[16,4,4096]{2,1,0:T(4,128)} %broadcast_in_dim.20), calls=%async_computation.3 | async-start | bytes 2097152 | tf_op jit(solution)/shard_map/all_to_all | solution.py:18
  190.7 8.6 %copy-start.2 = (f32[64,64,64]{2,0,1:T(8,128)S(1)}, f32[64,64,64]{2,0,1:T(8,128)}, u32[]{:S(2)}) copy-start(f32[64,64,64]{2,0,1:T(8,128)} %copy.44) | copy-start | bytes 3145732
  207.8 10.4 %all-to-all-start.5 = ((f32[16,1,1]{2,1,0:T(1,128)}), f32[16,1,1]{2,1,0:T(1,128)S(1)}, u32[]{:S(2)}, u32[]{:S(2)}) async-start(f32[16,1,1]{2,1,0:T(1,128)} %broadcast_in_dim.23), calls=%async_computation.5 | async-start | bytes 16384 | tf_op jit(solution)/shard_map/all_to_all | solution.py:18
where the time goes:
time: 225 us; the launch traced here: 222 us
  waiting for transfers between devices  99.5 us (44%)
  matrix products  48.1 us (21%)
  local copies, waits for them, and re-layouts  31.1 us (14%)
  starting transfers between devices  30.3 us (13%)
  other arithmetic  7.19 us (3%)
  between operations  5.5 us (2%)
    all_to_all x6, waiting for transfers between devices, copy_for_each(): lax.all_to_all(jnp.broadcast_to(x[None], (devices, *x.shape)), axis, 0, 0...  99.5 us
    all_to_all x6, starting transfers between devices, copy_for_each(): lax.all_to_all(jnp.broadcast_to(x[None], (devices, *x.shape)), axis, 0, 0...  30.3 us
    dot_general x3, matrix products, on_device(): jnp.einsum('bct,nst->nbcs', current, isometry, precision=PRECISE)  25.8 us
    dot_general x3, matrix products, on_device(): summed = jnp.einsum('abs,nbcs->nac', current, inner_sum, precision=PRECISE)  22.3 us
    transpose x5, local copies, waits for them, and re-layouts, on_device(): current = gathered.reshape(width, width, width).transpose(1, 2, 0)  14.2 us
    reshape x4, local copies, waits for them, and re-layouts, laid_out(): pieces.reshape(*dims[:dim], dims[dim] * dims[dim + 1], *dims[dim + 2:])  7.96 us
    broadcast_in_dim x6, local copies, waits for them, and re-layouts, copy_for_each(): jnp.broadcast_to(x[None], (devices, *x.shape))  6.91 us
  transfers between devices with their start and end apart: 6, of which 6 were waited for; matrix products, arithmetic and copies ran while one was open for 2% of the time, Pallas kernels for 0%

commit v1 on v0

v1 whole, which is shorter than its diff:
```python
import functools

import jax
import jax.numpy as jnp
from jax import lax
from jax.experimental import pallas as pl
from jax.experimental.pallas import tpu as pltpu
from jax.sharding import PartitionSpec as P

EPSILON = 1e-06
PIECES = 2
UNROLL = 8
F32 = jnp.float32
BF16 = jnp.bfloat16


def split(x):
    high = x.astype(BF16)
    return high, (x - high.astype(F32)).astype(BF16)


def interleave(x, y, low):
    kept = jnp.where(low, x, y)
    moved = pltpu.roll(jnp.where(low, y, x), 64, 1)
    return jnp.where(low, kept, moved), jnp.where(low, moved, kept)


def kernel(
    levels, parts, tensor_ref, iso_ref, out_ref, log_ref,
    gathered, peaks, own_peak, spread, rows, weights, flipped, left_op, inner_hi, inner_lo, turned,
    ring_send, ring_recv, pair_send, pair_recv, peak_send, peak_recv,
):
    me = lax.axis_index("bond")
    core = lax.rem(me, 2)
    chip = me // 2
    chips = parts // 2
    far = chips // 2
    rows_own, width2 = tensor_ref.shape
    half = width2 // 2
    wide = half // PIECES

    def slot_of(offset, core):
        return lax.rem(chip + offset + chips, chips) * 2 + core

    pair = chip * 2 + (1 - core)
    signs = (1 - 2 * (chip < 2).astype(jnp.int32), 2 * (chip < 2).astype(jnp.int32) - 1)

    peers = [slot_of(offset, core) for offset in (1, -1, 2, -2)] + [pair]
    barrier = pltpu.get_barrier_semaphore()
    for peer in peers:
        pl.semaphore_signal(barrier, inc=1, device_id={"bond": peer}, device_id_type=pl.DeviceIdType.MESH)
    pl.semaphore_wait(barrier, len(peers))

    def lanes_of(q):
        return pl.ds(q * wide if isinstance(q, int) else pl.multiple_of(q * wide, 128), wide)

    def remote(ref, send_sem, recv_sem, device):
        return pltpu.make_async_remote_copy(
            src_ref=ref,
            dst_ref=ref,
            send_sem=send_sem,
            recv_sem=recv_sem,
            device_id={"bond": device},
            device_id_type=pl.DeviceIdType.MESH,
        )

    def way_of(sign):
        return (1 - sign) // 2

    def ring_copy(level, sign, total, hops, i, offset):
        q = i + way_of(sign) * (PIECES // 2) if total == far else i
        ref = gathered.at[level, slot_of(offset, core), :, lanes_of(q)]
        way = way_of(sign)
        return remote(ref, ring_send.at[level, total - 1, way, i], ring_recv.at[level, total - 1, way, i], slot_of(sign * hops, core))

    def sending(level, sign, total, i):
        hops = total if total <= 2 else total - 2
        return ring_copy(level, sign, total, hops, i, sign * (hops - total))

    def arriving(level, sign, total, i):
        return ring_copy(level, sign, total, total if total <= 2 else total - 2, i, -sign * total)

    def count(total):
        return PIECES // 2 if total == far else PIECES

    def pair_copy(level, sign, total, i, sent):
        slot = slot_of(-sign * total, core if sent else 1 - core)
        q = i + way_of(sign) * (PIECES // 2) if total == far else i
        ref = gathered.at[level, slot, :, lanes_of(q)]
        way = 0 if total == 0 else way_of(sign)
        return remote(ref, pair_send.at[level, total, way, i], pair_recv.at[level, total, way, i], pair)

    def pair_block(level, sent):
        ref = gathered.at[level, me if sent else pair]
        return remote(ref, pair_send.at[level, 0, 0, 0], pair_recv.at[level, 0, 0, 0], pair)

    def start_gather(level):
        for total in (2, 1):
            for i in range(PIECES):
                for sign in (1, -1):
                    sending(level, sign, total, i).start()
        pair_block(level, True).start()

    def receive(level, sign, total):
        for i in range(count(total)):
            arriving(level, sign, total, i).wait_recv()
            pair_copy(level, sign, total, i, True).start()

    def pair_receive(level, total):
        for sign in (1, -1):
            for i in range(count(total)):
                pair_copy(level, sign, total, i, False).wait_recv()

    def near_gather(level):
        for sign in signs:
            for i in range(PIECES):
                arriving(level, sign, 2, i).wait_recv()
                sending(level, sign, 3, i).start()
                pair_copy(level, sign, 2, i, True).start()
            for i in range(count(far)):
                sending(level, sign, far, i).start()
        for sign in signs:
            receive(level, sign, 1)
        pair_block(level, False).wait_recv()
        pair_receive(level, 1)
        pair_receive(level, 2)

    def far_gather(level):
        for total in (3, far):
            for sign in signs:
                receive(level, sign, total)
        pair_receive(level, 3)
        pair_receive(level, far)

    def wait_sent(level):
        for total in range(1, far + 1):
            for sign in (1, -1):
                for i in range(count(total)):
                    sending(level, sign, total, i).wait_send()
                    pair_copy(level, sign, total, i, True).wait_send()
        pair_block(level, True).wait_send()

    def load_isometry(level):
        pairs = iso_ref.shape[2] // 128
        for n in range(rows_own):
            for j in range(pairs):
                spread[n * pairs + j : n * pairs + j + 1, :] = iso_ref[level, n : n + 1, j * 128 : (j + 1) * 128]
        for n in range(rows_own):
            both = spread[n * pairs : (n + 1) * pairs, :]
            rows[pl.ds(n * 2 * pairs, pairs, stride=2), :] = both
            rows[pl.ds(n * 2 * pairs + 1, pairs, stride=2), :] = pltpu.roll(both, 64, 1)
        hi, lo = split(rows[...][:, :64])
        left_op[:, :64] = hi
        left_op[:, 64:128] = hi
        left_op[:, 128:192] = lo

    low_lanes = lax.broadcasted_iota(jnp.int32, (64, 128), 1) < 64
    low_rows = lax.broadcasted_iota(jnp.int32, (8, 128), 0) < 4

    def contract(level, inverse):
        left_now = left_op[...]

        def first(i, _):
            lanes = pl.ds(pl.multiple_of(i * 128, 128), 128)
            top, bottom = [], []
            for d in range(0, parts, 2):
                x, y = gathered[level, d, :, lanes], gathered[level, d + 1, :, lanes]
                top.append(jnp.where(low_rows, x, pltpu.roll(y, 4, 0)))
                bottom.append(jnp.where(low_rows, pltpu.roll(x, 4, 0), y))
            both = jnp.concatenate(top + bottom, axis=0)
            if inverse is not None:
                both = both * inverse
            flipped[pl.ds(pl.multiple_of(i * 128, 128), 128), :] = both.T
            hi, lo = split(both)
            operand = jnp.concatenate(
                [jnp.concatenate([hi[h * 64 : h * 64 + 64], lo[h * 64 : h * 64 + 64], hi[h * 64 : h * 64 + 64]], axis=0) for h in (0, 1)],
                axis=1,
            )
            inner = jnp.dot(left_now, operand, preferred_element_type=F32)
            for h in (0, 1):
                for n in range(0, rows_own, 2):
                    x = inner[n * 64 : n * 64 + 64, h * 128 : h * 128 + 128]
                    y = inner[n * 64 + 64 : n * 64 + 128, h * 128 : h * 128 + 128]
                    for b, block in enumerate(interleave(x, y, low_lanes)):
                        place = pl.ds(pl.multiple_of(h * 2048 + i * 128, 128) + b * 64, 64)
                        hi, lo = split(block)
                        inner_hi[place, n * 64 : n * 64 + 128] = hi
                        inner_lo[place, n * 64 : n * 64 + 128] = lo
            return 0

        lax.fori_loop(0, half // 128, first, 0, unroll=UNROLL)

        low32 = low_lanes[:32]
        for j in range(32):
            x = flipped[pl.ds(2 * j, 32, stride=64), :]
            y = flipped[pl.ds(2 * j + 1, 32, stride=64), :]
            block = jnp.concatenate(interleave(x, y, low32), axis=0)
            hi, lo = split(block)
            weights[:64, j * 128 : j * 128 + 128] = hi
            weights[64:, j * 128 : j * 128 + 128] = lo

        main = jnp.dot(weights[...], inner_hi[...], preferred_element_type=F32)
        rest = jnp.dot(weights[:64, :], inner_lo[...], preferred_element_type=F32)
        return main[:64] + (main[64:] + rest)

    def own_layout(summed):
        rows[:64, :] = summed[:, :128]
        rows[64:128, :] = summed[:, 128:]
        for g in (0, 1):
            x = rows[pl.ds(g * 64, 32, stride=2), :]
            y = rows[pl.ds(g * 64 + 1, 32, stride=2), :]
            for b, block in enumerate(interleave(x, y, low_lanes[:32])):
                n = 2 * g + b
                turned[n * 16 : n * 16 + 16, :] = block[:16]
                turned[64 + n * 16 : 64 + n * 16 + 16, :] = block[16:]
        return [turned[pl.ds(j, 8, stride=16), :] for j in range(16)]

    def peak_over(level, offsets, peak):
        peaks = [peak] * 4
        for offset in offsets:
            for c in (0, 1):
                block = jnp.abs(gathered[level, slot_of(offset, c)])
                for j in range(half // 128):
                    peaks[j % 4] = jnp.maximum(peaks[j % 4], block[:, j * 128 : j * 128 + 128])
        return jnp.maximum(jnp.maximum(peaks[0], peaks[1]), jnp.maximum(peaks[2], peaks[3]))

    gathered[0, me] = jnp.concatenate([tensor_ref[:, :half], tensor_ref[:, half:]], axis=0)
    start_gather(0)
    log_density = jnp.zeros((1, 1), F32)
    for level in range(levels):
        load_isometry(level)
        near_gather(level)
        peak = jnp.zeros((8, 128), F32)
        if level > 0:
            peak = peak_over(level, range(-2, 3), peak)
        far_gather(level)
        inverse = None
        if level > 0:
            peak = peak_over(level, range(3, 6), peak)
            largest = jnp.max(jnp.max(peak, axis=0, keepdims=True), axis=1, keepdims=True) + EPSILON
            log_density = log_density + jnp.log(largest) * 0.5**level
            inverse = 1.0 / largest
        tiles = own_layout(contract(level, inverse))
        if level + 1 < levels:
            for j, tile in enumerate(tiles):
                gathered[level + 1, me, :, j * 128 : j * 128 + 128] = tile
            start_gather(level + 1)

    peak = functools.reduce(jnp.maximum, [jnp.abs(tile) for tile in tiles])
    own_peak[...] = peak
    peaks[me] = peak

    def peak_copy(d):
        return pltpu.make_async_remote_copy(
            src_ref=own_peak,
            dst_ref=peaks.at[me],
            send_sem=peak_send.at[d],
            recv_sem=peak_recv.at[d],
            device_id={"bond": lax.rem(me + d, parts)},
            device_id_type=pl.DeviceIdType.MESH,
        )

    def peak_arrival(d):
        return pltpu.make_async_remote_copy(
            src_ref=own_peak,
            dst_ref=peaks.at[lax.rem(me + parts - d, parts)],
            send_sem=peak_send.at[d],
            recv_sem=peak_recv.at[d],
            device_id={"bond": lax.rem(me + d, parts)},
            device_id_type=pl.DeviceIdType.MESH,
        )

    for d in range(1, parts):
        peak_copy(d).start()
    for level in range(levels):
        wait_sent(level)
    for d in range(1, parts):
        peak_arrival(d).wait_recv()
    peak = functools.reduce(jnp.maximum, [peaks[d] for d in range(parts)])
    largest = jnp.max(jnp.max(peak, axis=0, keepdims=True), axis=1, keepdims=True) + EPSILON
    log_density = log_density + jnp.log(largest) * 0.5**levels
    inverse = 1.0 / largest
    for j, tile in enumerate(tiles):
        tile = tile * inverse
        out_ref[:, j * 128 : j * 128 + 128] = tile[:4]
        out_ref[:, half + j * 128 : half + j * 128 + 128] = tile[4:]
    log_ref[...] = jnp.broadcast_to(log_density, log_ref.shape)
    for d in range(1, parts):
        peak_copy(d).wait_send()


def solution(mesh):
    parts = mesh.shape["bond"]

    def on_device(tensor, isometries):
        levels = isometries.shape[0]
        rows, width2 = tensor.shape
        width = rows * parts
        far = parts // 4
        dma = pltpu.SemaphoreType.DMA
        vmem = pl.BlockSpec(memory_space=pltpu.VMEM)
        out, log_density = pl.pallas_call(
            functools.partial(kernel, levels, parts),
            out_shape=(jax.ShapeDtypeStruct(tensor.shape, F32), jax.ShapeDtypeStruct((1, 128), F32)),
            in_specs=[vmem, vmem],
            out_specs=(vmem, vmem),
            scratch_shapes=[
                pltpu.VMEM((levels, parts, 2 * rows, width2 // 2), F32),
                pltpu.VMEM((parts, 8, 128), F32),
                pltpu.VMEM((8, 128), F32),
                pltpu.VMEM((rows * width // 2, 128), F32),
                pltpu.VMEM((rows * width, 128), F32),
                pltpu.VMEM((2 * width, width2), BF16),
                pltpu.VMEM((width2 // 2, 128), F32),
                pltpu.VMEM((rows * width, 3 * width), BF16),
                pltpu.VMEM((width2, rows * width), BF16),
                pltpu.VMEM((width2, rows * width), BF16),
                pltpu.VMEM((128, 128), F32),
                dma((levels, far, 2, PIECES)),
                dma((levels, far, 2, PIECES)),
                dma((levels, far + 1, 2, PIECES)),
                dma((levels, far + 1, 2, PIECES)),
                dma((parts,)),
                dma((parts,)),
            ],
            compiler_params=pltpu.CompilerParams(collective_id=0, has_side_effects=True),
        )(tensor, isometries)
        return out, log_density[0, :1]

    in_specs = (P(("temp", "bond"), None), P("temp", "bond", None))
    out_specs = (P(("temp", "bond"), None), P("temp"))
    return jax.shard_map(on_device, mesh=mesh, in_specs=in_specs, out_specs=out_specs, check_vma=False)
```

time: 225 us -> 65.6 us (0.29); the launches traced: 222 us -> 65.4 us
  waiting for transfers between devices: 99.5 us -> 0 us
  Pallas kernels: 0 us -> 62.1 us
  matrix products: 48.1 us -> 0 us
  starting transfers between devices: 30.3 us -> 0 us
  local copies, waits for them, and re-layouts: 31.1 us -> 1.48 us
  other arithmetic: 7.19 us -> 0 us
  between operations: 5.5 us -> 1.81 us
    all_to_all x6 -> x0, waiting for transfers between devices: 99.5 us -> none  [copy_for_each(): lax.all_to_all(jnp.broadcast_to(x[None], (devices, *x.shape)), axis, 0, 0...]
    pallas_call x0 -> x1, Pallas kernels: none -> 62.1 us  [on_device(): pl.pallas_call(functools.partial(kernel, levels, parts), out_shape=(jax.S...]
    dot_general x6 -> x0, matrix products: 48.1 us -> none  [the longest x3 25.8 us: on_device(): jnp.einsum('bct,nst->nbcs', current, isometry, precision=PRECISE)]
    all_to_all x6 -> x0, starting transfers between devices: 30.3 us -> none  [copy_for_each(): lax.all_to_all(jnp.broadcast_to(x[None], (devices, *x.shape)), axis, 0, 0...]
    transpose x5 -> x0, local copies, waits for them, and re-layouts: 14.2 us -> none  [on_device(): current = gathered.reshape(width, width, width).transpose(1, 2, 0)]
    reshape x4 -> x0, local copies, waits for them, and re-layouts: 7.96 us -> none  [laid_out(): pieces.reshape(*dims[:dim], dims[dim] * dims[dim + 1], *dims[dim + 2:])]
    broadcast_in_dim x8 -> x0, local copies, waits for them, and re-layouts: 7.06 us -> none  [the longest x6 6.91 us: copy_for_each(): jnp.broadcast_to(x[None], (devices, *x.shape))]
    transpose x2 -> x0, other arithmetic: 3.58 us -> none  [on_device(): current = gathered.reshape(width, width, width).transpose(1, 2, 0)]
  transfers between devices with their start and end apart: 6 -> 0, of which waited for: 6 -> 0; matrix products, arithmetic and copies ran while one was open for 2% -> 0% of each run, Pallas kernels for 0% -> 0%
where the time goes in v1:
time: 65.6 us; the launch traced here: 65.4 us
  Pallas kernels  62.1 us (95%)
  between operations  1.81 us (3%)
  local copies, waits for them, and re-layouts  1.48 us (2%)
    pallas_call x1, Pallas kernels, on_device(): pl.pallas_call(functools.partial(kernel, levels, parts), out_shape=(jax.S...  62.1 us
    unnamed x3, local copies, waits for them, and re-layouts  1.48 us

profile of v1, /device:TPU:1, one launch (start us, length us, event | category | flops | bytes accessed | tf_op | source)
XLA Modules:
  0.0 65.4 jit_solution(1048466914828623441)
XLA Ops:
  0.6 62.1 %shard_map.41 = (f32[4,4096]{1,0:T(4,128)}, f32[1,128]{1,0:T(1,128)}) custom-call(f32[4,4096]{1,0:T(4,128)} %tensor_ref.1, f32[3,4,4096]{2,1,0:T(4,128)} %iso_ref.1), custom_call_target="tpu_custom_call" | custom-call | tf_op jit(solution)/shard_map/pallas_call | solution.py:302
  62.8 0.0 copy-start
  62.8 1.5 %copy.6 = f32[4,4096]{1,0:T(4,128)} copy(f32[4,4096]{1,0:T(4,128)} %get-tuple-element.8) | data formatting | bytes 131072
  64.3 0.0 copy-done
Async XLA Ops:
  62.8 1.5 %copy-start = (f32[1,128]{1,0:T(1,128)S(1)}, f32[1,128]{1,0:T(1,128)}, u32[]{:S(2)}) copy-start(f32[1,128]{1,0:T(1,128)} %get-tuple-element.5) | copy-start | bytes 1540

commit v2 on v1

--- a/solution.py
+++ b/solution.py
@@ -26,10 +26,14 @@
 
 
 def kernel(
-    levels, parts, tensor_ref, iso_ref, out_ref, log_ref,
-    gathered, peaks, own_peak, spread, rows, weights, flipped, left_op, inner_hi, inner_lo, turned,
-    ring_send, ring_recv, pair_send, pair_recv, peak_send, peak_recv,
+    levels, parts, tensor_hbm, iso_hbm, out_ref, log_ref,
+    tensor_ref, iso_ref, gathered, peaks, own_peak, spread, rows, weights, flipped, left_op, inner_hi, inner_lo, turned,
+    ring_send, ring_recv, pair_send, pair_recv, peak_send, peak_recv, in_sem,
 ):
+    tensor_in = pltpu.make_async_copy(tensor_hbm, tensor_ref, in_sem.at[0])
+    iso_in = pltpu.make_async_copy(iso_hbm, iso_ref, in_sem.at[1])
+    tensor_in.start()
+    iso_in.start()
     me = lax.axis_index("bond")
     core = lax.rem(me, 2)
     chip = me // 2
@@ -49,9 +53,9 @@
     barrier = pltpu.get_barrier_semaphore()
     for peer in peers:
         pl.semaphore_signal(barrier, inc=1, device_id={"bond": peer}, device_id_type=pl.DeviceIdType.MESH)
-    pl.semaphore_wait(barrier, len(peers))
-
-    def lanes_of(q):
+
+    def lanes_of(sign, i):
+        q = lax.rem(i + way_of(sign) * (PIECES // 2), PIECES)
         return pl.ds(q * wide if isinstance(q, int) else pl.multiple_of(q * wide, 128), wide)
 
     def remote(ref, send_sem, recv_sem, device):
@@ -68,8 +72,9 @@
         return (1 - sign) // 2
 
     def ring_copy(level, sign, total, hops, i, offset):
-        q = i + way_of(sign) * (PIECES // 2) if total == far else i
-        ref = gathered.at[level, slot_of(offset, core), :, lanes_of(q)]
+        ref = gathered.at[level, slot_of(offset, core)]
+        if total in (2, far):
+            ref = ref.at[:, lanes_of(sign, i)]
         way = way_of(sign)
         return remote(ref, ring_send.at[level, total - 1, way, i], ring_recv.at[level, total - 1, way, i], slot_of(sign * hops, core))
 
@@ -81,12 +86,13 @@
         return ring_copy(level, sign, total, total if total <= 2 else total - 2, i, -sign * total)
 
     def count(total):
-        return PIECES // 2 if total == far else PIECES
+        return PIECES // 2 if total == far else PIECES if total == 2 else 1
 
     def pair_copy(level, sign, total, i, sent):
         slot = slot_of(-sign * total, core if sent else 1 - core)
-        q = i + way_of(sign) * (PIECES // 2) if total == far else i
-        ref = gathered.at[level, slot, :, lanes_of(q)]
+        ref = gathered.at[level, slot]
+        if total == far:
+            ref = ref.at[:, lanes_of(sign, i)]
         way = 0 if total == 0 else way_of(sign)
         return remote(ref, pair_send.at[level, total, way, i], pair_recv.at[level, total, way, i], pair)
 
@@ -96,7 +102,7 @@
 
     def start_gather(level):
         for total in (2, 1):
-            for i in range(PIECES):
+            for i in range(count(total)):
                 for sign in (1, -1):
                     sending(level, sign, total, i).start()
         pair_block(level, True).start()
@@ -108,17 +114,17 @@
 
     def pair_receive(level, total):
         for sign in (1, -1):
-            for i in range(count(total)):
+            for i in range(count(total) if total == far else 1):
                 pair_copy(level, sign, total, i, False).wait_recv()
 
     def near_gather(level):
         for sign in signs:
             for i in range(PIECES):
                 arriving(level, sign, 2, i).wait_recv()
-                sending(level, sign, 3, i).start()
-                pair_copy(level, sign, 2, i, True).start()
-            for i in range(count(far)):
-                sending(level, sign, far, i).start()
+                if i < count(far):
+                    sending(level, sign, far, i).start()
+            sending(level, sign, 3, 0).start()
+            pair_copy(level, sign, 2, 0, True).start()
         for sign in signs:
             receive(level, sign, 1)
         pair_block(level, False).wait_recv()
@@ -126,7 +132,7 @@
         pair_receive(level, 2)
 
     def far_gather(level):
-        for total in (3, far):
+        for total in (far, 3):
             for sign in signs:
                 receive(level, sign, total)
         pair_receive(level, 3)
@@ -137,6 +143,7 @@
             for sign in (1, -1):
                 for i in range(count(total)):
                     sending(level, sign, total, i).wait_send()
+                for i in range(count(total) if total == far else 1):
                     pair_copy(level, sign, total, i, True).wait_send()
         pair_block(level, True).wait_send()
 
@@ -150,15 +157,15 @@
             rows[pl.ds(n * 2 * pairs, pairs, stride=2), :] = both
             rows[pl.ds(n * 2 * pairs + 1, pairs, stride=2), :] = pltpu.roll(both, 64, 1)
         hi, lo = split(rows[...][:, :64])
-        left_op[:, :64] = hi
-        left_op[:, 64:128] = hi
-        left_op[:, 128:192] = lo
+        left_op[0, :, :64] = hi
+        left_op[0, :, 64:] = hi
+        left_op[1, :, :64] = lo
 
     low_lanes = lax.broadcasted_iota(jnp.int32, (64, 128), 1) < 64
     low_rows = lax.broadcasted_iota(jnp.int32, (8, 128), 0) < 4
 
     def contract(level, inverse):
-        left_now = left_op[...]
+        left_now = jnp.concatenate([left_op[0], left_op[1, :, :64]], axis=1)
 
         def first(i, _):
             lanes = pl.ds(pl.multiple_of(i * 128, 128), 128)
@@ -184,8 +191,8 @@
                     for b, block in enumerate(interleave(x, y, low_lanes)):
                         place = pl.ds(pl.multiple_of(h * 2048 + i * 128, 128) + b * 64, 64)
                         hi, lo = split(block)
-                        inner_hi[place, n * 64 : n * 64 + 128] = hi
-                        inner_lo[place, n * 64 : n * 64 + 128] = lo
+                        inner_hi[n // 2, place, :] = hi
+                        inner_lo[n // 2, place, :] = lo
             return 0
 
         lax.fori_loop(0, half // 128, first, 0, unroll=UNROLL)
@@ -196,11 +203,12 @@
             y = flipped[pl.ds(2 * j + 1, 32, stride=64), :]
             block = jnp.concatenate(interleave(x, y, low32), axis=0)
             hi, lo = split(block)
-            weights[:64, j * 128 : j * 128 + 128] = hi
-            weights[64:, j * 128 : j * 128 + 128] = lo
-
-        main = jnp.dot(weights[...], inner_hi[...], preferred_element_type=F32)
-        rest = jnp.dot(weights[:64, :], inner_lo[...], preferred_element_type=F32)
+            weights[j, :64, :] = hi
+            weights[j, 64:, :] = lo
+
+        both = jnp.concatenate([weights[j] for j in range(32)], axis=1)
+        main = jnp.dot(both, jnp.concatenate([inner_hi[0], inner_hi[1]], axis=1), preferred_element_type=F32)
+        rest = jnp.dot(both[:64], jnp.concatenate([inner_lo[0], inner_lo[1]], axis=1), preferred_element_type=F32)
         return main[:64] + (main[64:] + rest)
 
     def own_layout(summed):
@@ -224,8 +232,11 @@
                     peaks[j % 4] = jnp.maximum(peaks[j % 4], block[:, j * 128 : j * 128 + 128])
         return jnp.maximum(jnp.maximum(peaks[0], peaks[1]), jnp.maximum(peaks[2], peaks[3]))
 
+    tensor_in.wait()
     gathered[0, me] = jnp.concatenate([tensor_ref[:, :half], tensor_ref[:, half:]], axis=0)
+    pl.semaphore_wait(barrier, len(peers))
     start_gather(0)
+    iso_in.wait()
     log_density = jnp.zeros((1, 1), F32)
     for level in range(levels):
         load_isometry(level)
@@ -247,6 +258,7 @@
             start_gather(level + 1)
 
     peak = functools.reduce(jnp.maximum, [jnp.abs(tile) for tile in tiles])
+    peak = jnp.max(peak, axis=0, keepdims=True)
     own_peak[...] = peak
     peaks[me] = peak
 
@@ -277,7 +289,7 @@
     for d in range(1, parts):
         peak_arrival(d).wait_recv()
     peak = functools.reduce(jnp.maximum, [peaks[d] for d in range(parts)])
-    largest = jnp.max(jnp.max(peak, axis=0, keepdims=True), axis=1, keepdims=True) + EPSILON
+    largest = jnp.max(peak, axis=1, keepdims=True) + EPSILON
     log_density = log_density + jnp.log(largest) * 0.5**levels
     inverse = 1.0 / largest
     for j, tile in enumerate(tiles):
@@ -302,19 +314,21 @@
         out, log_density = pl.pallas_call(
             functools.partial(kernel, levels, parts),
             out_shape=(jax.ShapeDtypeStruct(tensor.shape, F32), jax.ShapeDtypeStruct((1, 128), F32)),
-            in_specs=[vmem, vmem],
+            in_specs=[pl.BlockSpec(memory_space=pl.ANY)] * 2,
             out_specs=(vmem, vmem),
             scratch_shapes=[
+                pltpu.VMEM(tensor.shape, F32),
+                pltpu.VMEM(isometries.shape, F32),
                 pltpu.VMEM((levels, parts, 2 * rows, width2 // 2), F32),
-                pltpu.VMEM((parts, 8, 128), F32),
-                pltpu.VMEM((8, 128), F32),
+                pltpu.VMEM((parts, 1, 128), F32),
+                pltpu.VMEM((1, 128), F32),
                 pltpu.VMEM((rows * width // 2, 128), F32),
                 pltpu.VMEM((rows * width, 128), F32),
-                pltpu.VMEM((2 * width, width2), BF16),
+                pltpu.VMEM((width // 2, 2 * width, 128), BF16),
                 pltpu.VMEM((width2 // 2, 128), F32),
-                pltpu.VMEM((rows * width, 3 * width), BF16),
-                pltpu.VMEM((width2, rows * width), BF16),
-                pltpu.VMEM((width2, rows * width), BF16),
+                pltpu.VMEM((2, rows * width, 128), BF16),
+                pltpu.VMEM((rows // 2, width2, 128), BF16),
+                pltpu.VMEM((rows // 2, width2, 128), BF16),
                 pltpu.VMEM((128, 128), F32),
                 dma((levels, far, 2, PIECES)),
                 dma((levels, far, 2, PIECES)),
@@ -322,6 +336,7 @@
                 dma((levels, far + 1, 2, PIECES)),
                 dma((parts,)),
                 dma((parts,)),
+                dma((2,)),
             ],
             compiler_params=pltpu.CompilerParams(collective_id=0, has_side_effects=True),
         )(tensor, isometries)

time: 65.6 us -> 62.5 us (0.953)
  Pallas kernels: 62.1 us -> 59 us
    pallas_call x1, Pallas kernels: 62.1 us -> 59 us  [on_device(): pl.pallas_call(functools.partial(kernel, levels, parts), out_shape=(jax.S...]
where the time goes in v2:
time: 62.5 us; the launch traced here: 62.3 us
  Pallas kernels  59 us (94%)
  between operations  1.81 us (3%)
  local copies, waits for them, and re-layouts  1.48 us (2%)
    pallas_call x1, Pallas kernels, on_device(): pl.pallas_call(functools.partial(kernel, levels, parts), out_shape=(jax.S...  59 us
    unnamed x3, local copies, waits for them, and re-layouts  1.48 us

profile of v2, /device:TPU:1, one launch (start us, length us, event | category | flops | bytes accessed | tf_op | source)
XLA Modules:
  0.0 62.3 jit_solution(16918269583007174997)
XLA Ops:
  0.6 59.0 %shard_map.41 = (f32[4,4096]{1,0:T(4,128)}, f32[1,128]{1,0:T(1,128)}) custom-call(f32[4,4096]{1,0:T(4,128)} %tensor_hbm.1, f32[3,4,4096]{2,1,0:T(4,128)} %iso_hbm.1), custom_call_target="tpu_custom_call" | custom-call | tf_op jit(solution)/shard_map/pallas_call | solution.py:314
  59.7 0.0 copy-start
  59.7 1.5 %copy.6 = f32[4,4096]{1,0:T(4,128)} copy(f32[4,4096]{1,0:T(4,128)} %get-tuple-element.8) | data formatting | bytes 131072
  61.2 0.0 copy-done
Async XLA Ops:
  59.7 1.5 %copy-start = (f32[1,128]{1,0:T(1,128)S(1)}, f32[1,128]{1,0:T(1,128)}, u32[]{:S(2)}) copy-start(f32[1,128]{1,0:T(1,128)} %get-tuple-element.5) | copy-start | bytes 1540

commit v3 on v2

--- a/solution.py
+++ b/solution.py
@@ -28,7 +28,7 @@
 def kernel(
     levels, parts, tensor_hbm, iso_hbm, out_ref, log_ref,
     tensor_ref, iso_ref, gathered, peaks, own_peak, spread, rows, weights, flipped, left_op, inner_hi, inner_lo, turned,
-    ring_send, ring_recv, pair_send, pair_recv, peak_send, peak_recv, in_sem,
+    ring_recv, pair_recv, sent_sem, peak_send, peak_recv, in_sem,
 ):
     tensor_in = pltpu.make_async_copy(tensor_hbm, tensor_ref, in_sem.at[0])
     iso_in = pltpu.make_async_copy(iso_hbm, iso_ref, in_sem.at[1])
@@ -76,7 +76,8 @@
         if total in (2, far):
             ref = ref.at[:, lanes_of(sign, i)]
         way = way_of(sign)
-        return remote(ref, ring_send.at[level, total - 1, way, i], ring_recv.at[level, total - 1, way, i], slot_of(sign * hops, core))
+        place = (0, 1, 3, 4)[total - 1] + i
+        return remote(ref, sent_sem.at[level], ring_recv.at[level, way, place], slot_of(sign * hops, core))
 
     def sending(level, sign, total, i):
         hops = total if total <= 2 else total - 2
@@ -93,12 +94,11 @@
         ref = gathered.at[level, slot]
         if total == far:
             ref = ref.at[:, lanes_of(sign, i)]
-        way = 0 if total == 0 else way_of(sign)
-        return remote(ref, pair_send.at[level, total, way, i], pair_recv.at[level, total, way, i], pair)
+        return remote(ref, sent_sem.at[level], pair_recv.at[level, total // 3], pair)
 
     def pair_block(level, sent):
         ref = gathered.at[level, me if sent else pair]
-        return remote(ref, pair_send.at[level, 0, 0, 0], pair_recv.at[level, 0, 0, 0], pair)
+        return remote(ref, sent_sem.at[level], pair_recv.at[level, 0], pair)
 
     def start_gather(level):
         for total in (2, 1):
@@ -112,10 +112,9 @@
             arriving(level, sign, total, i).wait_recv()
             pair_copy(level, sign, total, i, True).start()
 
-    def pair_receive(level, total):
-        for sign in (1, -1):
-            for i in range(count(total) if total == far else 1):
-                pair_copy(level, sign, total, i, False).wait_recv()
+    def pair_receive(level, part):
+        blocks = gathered.at[level, pl.ds(0, (5, 3)[part])]
+        remote(blocks, sent_sem.at[level], pair_recv.at[level, part], pair).wait_recv()
 
     def near_gather(level):
         for sign in signs:
@@ -127,25 +126,17 @@
             pair_copy(level, sign, 2, 0, True).start()
         for sign in signs:
             receive(level, sign, 1)
-        pair_block(level, False).wait_recv()
-        pair_receive(level, 1)
-        pair_receive(level, 2)
+        pair_receive(level, 0)
 
     def far_gather(level):
         for total in (far, 3):
             for sign in signs:
                 receive(level, sign, total)
-        pair_receive(level, 3)
-        pair_receive(level, far)
+        pair_receive(level, 1)
 
     def wait_sent(level):
-        for total in range(1, far + 1):
-            for sign in (1, -1):
-                for i in range(count(total)):
-                    sending(level, sign, total, i).wait_send()
-                for i in range(count(total) if total == far else 1):
-                    pair_copy(level, sign, total, i, True).wait_send()
-        pair_block(level, True).wait_send()
+        blocks = gathered.at[level, pl.ds(0, 15)]
+        remote(blocks, sent_sem.at[level], pair_recv.at[level, 0], pair).wait_send()
 
     def load_isometry(level):
         pairs = iso_ref.shape[2] // 128
@@ -259,35 +250,26 @@
 
     peak = functools.reduce(jnp.maximum, [jnp.abs(tile) for tile in tiles])
     peak = jnp.max(peak, axis=0, keepdims=True)
-    own_peak[...] = peak
+    own_peak[0] = peak
     peaks[me] = peak
 
-    def peak_copy(d):
+    def peak_copy(src, dst, d):
         return pltpu.make_async_remote_copy(
-            src_ref=own_peak,
-            dst_ref=peaks.at[me],
-            send_sem=peak_send.at[d],
-            recv_sem=peak_recv.at[d],
+            src_ref=src,
+            dst_ref=dst,
+            send_sem=peak_send.at[0],
+            recv_sem=peak_recv.at[0],
             device_id={"bond": lax.rem(me + d, parts)},
             device_id_type=pl.DeviceIdType.MESH,
         )
 
-    def peak_arrival(d):
-        return pltpu.make_async_remote_copy(
-            src_ref=own_peak,
-            dst_ref=peaks.at[lax.rem(me + parts - d, parts)],
-            send_sem=peak_send.at[d],
-            recv_sem=peak_recv.at[d],
-            device_id={"bond": lax.rem(me + d, parts)},
-            device_id_type=pl.DeviceIdType.MESH,
-        )
-
-    for d in range(1, parts):
-        peak_copy(d).start()
+    for d in sorted(range(1, parts), key=lambda d: -min(d, parts - d)):
+        peak_copy(own_peak.at[0], peaks.at[me], d).start()
+    others = peaks.at[pl.ds(0, parts - 1)]
+    peak_copy(others, others, 1).wait_send()
     for level in range(levels):
         wait_sent(level)
-    for d in range(1, parts):
-        peak_arrival(d).wait_recv()
+    peak_copy(others, others, 1).wait_recv()
     peak = functools.reduce(jnp.maximum, [peaks[d] for d in range(parts)])
     largest = jnp.max(peak, axis=1, keepdims=True) + EPSILON
     log_density = log_density + jnp.log(largest) * 0.5**levels
@@ -297,8 +279,6 @@
         out_ref[:, j * 128 : j * 128 + 128] = tile[:4]
         out_ref[:, half + j * 128 : half + j * 128 + 128] = tile[4:]
     log_ref[...] = jnp.broadcast_to(log_density, log_ref.shape)
-    for d in range(1, parts):
-        peak_copy(d).wait_send()
 
 
 def solution(mesh):
@@ -321,7 +301,7 @@
                 pltpu.VMEM(isometries.shape, F32),
                 pltpu.VMEM((levels, parts, 2 * rows, width2 // 2), F32),
                 pltpu.VMEM((parts, 1, 128), F32),
-                pltpu.VMEM((1, 128), F32),
+                pltpu.VMEM((1, 1, 128), F32),
                 pltpu.VMEM((rows * width // 2, 128), F32),
                 pltpu.VMEM((rows * width, 128), F32),
                 pltpu.VMEM((width // 2, 2 * width, 128), BF16),
@@ -330,12 +310,11 @@
                 pltpu.VMEM((rows // 2, width2, 128), BF16),
                 pltpu.VMEM((rows // 2, width2, 128), BF16),
                 pltpu.VMEM((128, 128), F32),
-                dma((levels, far, 2, PIECES)),
-                dma((levels, far, 2, PIECES)),
-                dma((levels, far + 1, 2, PIECES)),
-                dma((levels, far + 1, 2, PIECES)),
-                dma((parts,)),
-                dma((parts,)),
+                dma((levels, 2, far + 1)),
+                dma((levels, 2)),
+                dma((levels,)),
+                dma((1,)),
+                dma((1,)),
                 dma((2,)),
             ],
             compiler_params=pltpu.CompilerParams(collective_id=0, has_side_effects=True),

time: 62.5 us -> 60.6 us (0.970)
  Pallas kernels: 59 us -> 57.1 us
    pallas_call x1, Pallas kernels: 59 us -> 57.1 us  [on_device(): pl.pallas_call(functools.partial(kernel, levels, parts), out_shape=(jax.S...]
where the time goes in v3:
time: 60.6 us; the launch traced here: 60.4 us
  Pallas kernels  57.1 us (94%)
  between operations  1.81 us (3%)
  local copies, waits for them, and re-layouts  1.48 us (2%)
    pallas_call x1, Pallas kernels, on_device(): pl.pallas_call(functools.partial(kernel, levels, parts), out_shape=(jax.S...  57.1 us
    unnamed x3, local copies, waits for them, and re-layouts  1.48 us

profile of v3, /device:TPU:1, one launch (start us, length us, event | category | flops | bytes accessed | tf_op | source)
XLA Modules:
  0.0 60.4 jit_solution(10416712808202164779)
XLA Ops:
  0.6 57.1 %shard_map.41 = (f32[4,4096]{1,0:T(4,128)}, f32[1,128]{1,0:T(1,128)}) custom-call(f32[4,4096]{1,0:T(4,128)} %tensor_hbm.1, f32[3,4,4096]{2,1,0:T(4,128)} %iso_hbm.1), custom_call_target="tpu_custom_call" | custom-call | tf_op jit(solution)/shard_map/pallas_call | solution.py:294
  57.8 0.0 copy-start
  57.8 1.5 %copy.6 = f32[4,4096]{1,0:T(4,128)} copy(f32[4,4096]{1,0:T(4,128)} %get-tuple-element.8) | data formatting | bytes 131072
  59.2 0.0 copy-done
Async XLA Ops:
  57.8 1.5 %copy-start = (f32[1,128]{1,0:T(1,128)S(1)}, f32[1,128]{1,0:T(1,128)}, u32[]{:S(2)}) copy-start(f32[1,128]{1,0:T(1,128)} %get-tuple-element.5) | copy-start | bytes 1540

commit v4 on v3

--- a/solution.py
+++ b/solution.py
@@ -73,10 +73,10 @@
 
     def ring_copy(level, sign, total, hops, i, offset):
         ref = gathered.at[level, slot_of(offset, core)]
-        if total in (2, far):
+        if total > 1:
             ref = ref.at[:, lanes_of(sign, i)]
         way = way_of(sign)
-        place = (0, 1, 3, 4)[total - 1] + i
+        place = (0, 1, 1 + PIECES, 1 + 2 * PIECES)[total - 1] + i
         return remote(ref, sent_sem.at[level], ring_recv.at[level, way, place], slot_of(sign * hops, core))
 
     def sending(level, sign, total, i):
@@ -87,12 +87,12 @@
         return ring_copy(level, sign, total, total if total <= 2 else total - 2, i, -sign * total)
 
     def count(total):
-        return PIECES // 2 if total == far else PIECES if total == 2 else 1
+        return PIECES // 2 if total == far else 1 if total == 1 else PIECES
 
     def pair_copy(level, sign, total, i, sent):
         slot = slot_of(-sign * total, core if sent else 1 - core)
         ref = gathered.at[level, slot]
-        if total == far:
+        if total > 2:
             ref = ref.at[:, lanes_of(sign, i)]
         return remote(ref, sent_sem.at[level], pair_recv.at[level, total // 3], pair)
 
@@ -122,7 +122,7 @@
                 arriving(level, sign, 2, i).wait_recv()
                 if i < count(far):
                     sending(level, sign, far, i).start()
-            sending(level, sign, 3, 0).start()
+                sending(level, sign, 3, i).start()
             pair_copy(level, sign, 2, 0, True).start()
         for sign in signs:
             receive(level, sign, 1)
@@ -310,7 +310,7 @@
                 pltpu.VMEM((rows // 2, width2, 128), BF16),
                 pltpu.VMEM((rows // 2, width2, 128), BF16),
                 pltpu.VMEM((128, 128), F32),
-                dma((levels, 2, far + 1)),
+                dma((levels, 2, 1 + 2 * PIECES + PIECES // 2)),
                 dma((levels, 2)),
                 dma((levels,)),
                 dma((1,)),

time: 60.6 us -> 60.3 us (level)
  no operation moved by 1% of the time
where the time goes in v4:
time: 60.3 us; the launch traced here: 60.1 us
  Pallas kernels  56.8 us (94%)
  between operations  1.81 us (3%)
  local copies, waits for them, and re-layouts  1.48 us (2%)
    pallas_call x1, Pallas kernels, on_device(): pl.pallas_call(functools.partial(kernel, levels, parts), out_shape=(jax.S...  56.8 us
    unnamed x3, local copies, waits for them, and re-layouts  1.48 us

profile of v4, /device:TPU:1, one launch (start us, length us, event | category | flops | bytes accessed | tf_op | source)
XLA Modules:
  0.0 60.1 jit_solution(5378999797578808341)
XLA Ops:
  0.6 56.8 %shard_map.41 = (f32[4,4096]{1,0:T(4,128)}, f32[1,128]{1,0:T(1,128)}) custom-call(f32[4,4096]{1,0:T(4,128)} %tensor_hbm.1, f32[3,4,4096]{2,1,0:T(4,128)} %iso_hbm.1), custom_call_target="tpu_custom_call" | custom-call | tf_op jit(solution)/shard_map/pallas_call | solution.py:294
  57.4 0.0 copy-start
  57.4 1.5 %copy.6 = f32[4,4096]{1,0:T(4,128)} copy(f32[4,4096]{1,0:T(4,128)} %get-tuple-element.8) | data formatting | bytes 131072
  58.9 0.0 copy-done
Async XLA Ops:
  57.4 1.5 %copy-start = (f32[1,128]{1,0:T(1,128)S(1)}, f32[1,128]{1,0:T(1,128)}, u32[]{:S(2)}) copy-start(f32[1,128]{1,0:T(1,128)} %get-tuple-element.5) | copy-start | bytes 1540

commit v5 on v4

--- a/solution.py
+++ b/solution.py
@@ -8,7 +8,7 @@
 from jax.sharding import PartitionSpec as P
 
 EPSILON = 1e-06
-PIECES = 2
+PIECES = 4
 UNROLL = 8
 F32 = jnp.float32
 BF16 = jnp.bfloat16

time: 60.3 us -> 60.4 us (level)
  no operation moved by 1% of the time
where the time goes in v5:
time: 60.4 us; the launch traced here: 60.3 us
  Pallas kernels  57 us (94%)
  between operations  1.81 us (3%)
  local copies, waits for them, and re-layouts  1.48 us (2%)
    pallas_call x1, Pallas kernels, on_device(): pl.pallas_call(functools.partial(kernel, levels, parts), out_shape=(jax.S...  57 us
    unnamed x3, local copies, waits for them, and re-layouts  1.48 us

profile of v5, /device:TPU:1, one launch (start us, length us, event | category | flops | bytes accessed | tf_op | source)
XLA Modules:
  0.0 60.3 jit_solution(8841966995241881124)
XLA Ops:
  0.6 57.0 %shard_map.41 = (f32[4,4096]{1,0:T(4,128)}, f32[1,128]{1,0:T(1,128)}) custom-call(f32[4,4096]{1,0:T(4,128)} %tensor_hbm.1, f32[3,4,4096]{2,1,0:T(4,128)} %iso_hbm.1), custom_call_target="tpu_custom_call" | custom-call | tf_op jit(solution)/shard_map/pallas_call | solution.py:294
  57.6 0.0 copy-start
  57.6 1.5 %copy.6 = f32[4,4096]{1,0:T(4,128)} copy(f32[4,4096]{1,0:T(4,128)} %get-tuple-element.8) | data formatting | bytes 131072
  59.1 0.0 copy-done
Async XLA Ops:
  57.6 1.5 %copy-start = (f32[1,128]{1,0:T(1,128)S(1)}, f32[1,128]{1,0:T(1,128)}, u32[]{:S(2)}) copy-start(f32[1,128]{1,0:T(1,128)} %get-tuple-element.5) | copy-start | bytes 1540
